TPU v7x, 128 devices: a whole 4x4x4 slice. The times are simulated.
128 devices in a mesh: row: 16 (over y, z_lo, core), col: 8 (over x, z_hi).
Axes of the slice: x: 4, y: 4, z: 4 (z_hi: 2, z_lo: 2; z = z_hi * 2 + z_lo), core: 2. Of those that a mesh axis runs over, the one named last changes fastest.
Arguments:
- record: bfloat16 [6, 2048, 2560], P(None, ('row', 'col')), may hold values from -6 to 6
- taps: float32 [200], replicated, may hold values from -0.4375 to 0.4375
- plan: int32 [6], replicated, may hold values from 0 to 5, each once
- quality: int32 [2048], P(('row', 'col')), may hold values 0 or 1
Outputs:
- correlation: float32 [51, 2048, 2048], P(None, 'row', 'col')
Inputs may be any that keep to these rules, and one draw needn't show every extreme that they name: plan is a permutation of the recorded sub-windows; its first 4 entries name the ones that are stacked.
All inputs are finite; a program needn't handle non-finite values. No bound on the sum of `quality` on one device may be relied on, other than what follows from the above.
Results may differ from a plain program's by a relative error of at most 0.0039.
Values may be sent and summed in bfloat16 or wider, within the bound.
No kernel may reach another device: no remote copies, remote signals or barrier semaphores. Data moves between devices by JAX's collectives and lax.ppermute only.
A program may use at most 64 MiB of HBM per device.

v0:
```python
import math

import jax
import jax.numpy as jnp
from jax import lax
from jax.experimental import pallas as pl
from jax.experimental.pallas import tpu as pltpu
from jax.sharding import PartitionSpec as P


STRIDE = 20
TAPS = 200
HALFWIN = 32
MAXLAG = 25
SUB = 4
LAGS = 51
FRAMES = 128
SEGMENT = 32 * STRIDE
SPAN = 896
AXES = ("row", "col")
GROUP = 3


def whiten_kernel(plan_ref, record_ref, taps_ref, quality_ref, out_ref, samples, sems):
    chans = out_ref.shape[0]
    f32, bf16 = jnp.float32, jnp.bfloat16
    raw = record_ref.shape[2]

    def copy(s):
        return pltpu.make_async_copy(
            record_ref.at[plan_ref[s]], samples.at[s, :, pl.ds(0, raw)], sems.at[s]
        )

    for s in range(SUB):
        copy(s).start()
    samples[:, :, raw:] = jnp.zeros((SUB, chans, samples.shape[2] - raw), bf16)
    taps = taps_ref[...].reshape(1, TAPS)
    table = jnp.broadcast_to(
        jnp.concatenate([taps, jnp.zeros((1, SPAN - TAPS), f32)], axis=1), (32, SPAN)
    )
    k = lax.broadcasted_iota(jnp.int32, (32, SPAN), 0)
    for bit in range(5):
        moved = pltpu.roll(table, STRIDE << bit, 1)
        table = jnp.where((k >> bit) & 1 == 1, moved, table)
    high = table.astype(bf16)
    low = (table - high.astype(f32)).astype(bf16)
    filters = jnp.concatenate([high] * 4 + [low] * 4, axis=0)
    i = lax.broadcasted_iota(jnp.int32, (2 * FRAMES, FRAMES), 0) & (FRAMES - 1)
    j = lax.broadcasted_iota(jnp.int32, (2 * FRAMES, FRAMES), 1)
    band = jnp.where(jnp.abs(i - j) <= HALFWIN, 1.0, 0.0).astype(bf16)
    a = lax.broadcasted_iota(jnp.int32, (chans, chans), 0)
    b = lax.broadcasted_iota(jnp.int32, (chans, chans), 1)
    across = jnp.broadcast_to(
        quality_ref[...].reshape(1, chans).astype(f32), (chans, chans)
    )
    quality = jnp.sum(jnp.where(a == b, across, 0.0), axis=1, keepdims=True)
    for s in range(SUB):
        copy(s).wait()
    both = lax.dot_general(
        jnp.concatenate(
            [
                samples[s, :, b * SEGMENT : b * SEGMENT + SPAN]
                for s in range(SUB)
                for b in range(4)
            ],
            axis=0,
        ),
        filters,
        (((1,), (1,)), ((), ())),
        preferred_element_type=f32,
    )
    both = both[:, :FRAMES] + both[:, FRAMES:]
    lane = lax.broadcasted_iota(jnp.int32, (chans, FRAMES), 1)
    rows = []
    for s in range(SUB):
        p = [both[(s * 4 + b) * chans : (s * 4 + b + 1) * chans] for b in range(4)]
        rows.append(
            jnp.where(
                lane < 64,
                jnp.where(lane < 32, p[0], p[1]),
                jnp.where(lane < 96, p[2], p[3]),
            )
        )
    decimated = jnp.concatenate(rows, axis=0)
    size = jnp.abs(decimated)
    size_high = size.astype(bf16)
    size_low = (size - size_high.astype(f32)).astype(bf16)
    envelope = jnp.dot(
        jnp.concatenate([size_high, size_low], axis=1), band, preferred_element_type=f32
    ) * (1.0 / (2 * HALFWIN + 1))
    for s in range(SUB):
        d = decimated[s * chans : (s + 1) * chans]
        e = envelope[s * chans : (s + 1) * chans]
        out_ref[:, s * FRAMES : (s + 1) * FRAMES] = (d / (e + 1e-05) * quality).astype(bf16)


def whiten(record, taps, plan, quality):
    chans, raw = record.shape[1:]
    return pl.pallas_call(
        whiten_kernel,
        name="whiten",
        out_shape=jax.ShapeDtypeStruct((chans, SUB * FRAMES), jnp.bfloat16),
        in_specs=[
            pl.BlockSpec(memory_space=pltpu.SMEM),
            pl.BlockSpec(memory_space=pltpu.HBM),
            pl.BlockSpec(memory_space=pltpu.VMEM),
            pl.BlockSpec(memory_space=pltpu.VMEM),
        ],
        out_specs=pl.BlockSpec(memory_space=pltpu.VMEM),
        scratch_shapes=[
            pltpu.VMEM((SUB, chans, raw + SPAN - SEGMENT), jnp.bfloat16),
            pltpu.SemaphoreType.DMA((SUB,)),
        ],
        compiler_params=pltpu.CompilerParams(vmem_limit_bytes=8 << 20),
        cost_estimate=pl.CostEstimate(flops=1 << 28, bytes_accessed=1 << 19, transcendentals=0),
    )(*(pltpu.with_memory_space_constraint(v, pltpu.HBM) for v in (plan, record, taps, quality)))


S_MASKS = (1, 4, 2)


def spread(index, *masks):
    place = 0
    for bit, mask in enumerate(masks):
        if index >> bit & 1:
            place = place ^ mask
    return place


def correlate_kernel(s0_ref, s1_ref, r0_ref, r1_ref, out_ref, source, receiver, products, sems):
    count, length = source.shape
    chans = count // 8
    col, row = lax.axis_index("col"), lax.axis_index("row")
    for t in range(8):
        place = col ^ spread(t, *S_MASKS)
        part = (s0_ref, s1_ref)[t // 4]
        source[pl.ds(pl.multiple_of(place * chans, chans), chans)] = part[
            t % 4 * chans : (t % 4 + 1) * chans
        ].astype(jnp.float32)
    for half in range(2):
        core = (row & 1) ^ half
        part = (r0_ref, r1_ref)[half]
        for t in range(4):
            place = (row >> 1) ^ (4 - 2 * core) ^ spread(t, 2 - core, 1 + core)
            for j in range(2):
                start = ((core ^ j) * 8 + place) * chans
                receiver[pl.ds(pl.multiple_of(start, chans), chans)] = part[
                    (t * 2 + j) * chans : (t * 2 + j + 1) * chans
                ]
    turned = receiver[...].T
    lane = lax.broadcasted_iota(jnp.int32, (count, FRAMES), 1)
    scale = 1.0 / math.sqrt(length)

    def copy(g):
        part = pl.ds(g * GROUP, GROUP)
        return pltpu.make_async_copy(products.at[part], out_ref.at[part], sems.at[g])

    for g in range(LAGS // GROUP):
        moved = []
        for q in range(g * GROUP, (g + 1) * GROUP):
            shift = q - MAXLAG
            inside = (lane >= shift) & (lane < shift + FRAMES)
            moved.append(
                jnp.concatenate(
                    [
                        jnp.where(
                            inside,
                            pltpu.roll(
                                source[:, s * FRAMES : (s + 1) * FRAMES], shift % FRAMES, 1
                            ),
                            0.0,
                        ).astype(jnp.bfloat16)
                        for s in range(SUB)
                    ],
                    axis=1,
                )
            )
        product = jnp.dot(
            jnp.concatenate(moved, axis=0), turned, preferred_element_type=jnp.float32
        )
        products[g * GROUP : (g + 1) * GROUP] = (product * scale).reshape(GROUP, count, -1)
        copy(g).start()
    for g in range(LAGS // GROUP):
        copy(g).wait()


def correlate(*parts):
    count, width = 2 * parts[0].shape[0], 2 * parts[2].shape[0]
    length = parts[0].shape[1]
    whole = pl.BlockSpec(memory_space=pltpu.VMEM)
    return pl.pallas_call(
        correlate_kernel,
        name="correlate",
        out_shape=jax.ShapeDtypeStruct((LAGS, count, width), jnp.float32),
        in_specs=[whole] * 4,
        out_specs=pl.BlockSpec(memory_space=pl.ANY),
        scratch_shapes=[
            pltpu.VMEM((count, length), jnp.float32),
            pltpu.VMEM((width, length), jnp.bfloat16),
            pltpu.VMEM((LAGS, count, width), jnp.float32),
            pltpu.SemaphoreType.DMA((LAGS // GROUP,)),
        ],
        compiler_params=pltpu.CompilerParams(vmem_limit_bytes=24 << 20),
        cost_estimate=pl.CostEstimate(flops=1 << 31, bytes_accessed=1 << 23, transcendentals=0),
    )(*parts)


def send(block, target):
    pairs = [
        (row * 8 + col, target(row, col)[0] * 8 + target(row, col)[1])
        for row in range(16)
        for col in range(8)
    ]
    return lax.ppermute(block, AXES, pairs)


def to_column(row, col):
    y, z_lo, core = row >> 2, row >> 1 & 1, row & 1
    x, z_hi = col >> 1, col & 1
    return (x ^ 2 - core) * 4 + z_hi * 2 + core, y * 2 + z_lo


def join(*blocks):
    return jnp.concatenate(blocks, axis=0)


def body(record, taps, plan, quality):
    own = whiten(record, taps, plan, quality)
    both = join(own, send(own, lambda row, col: (row ^ 1, col)))
    other = send(own, lambda row, col: (row, col ^ S_MASKS[0]))
    receiver = send(both, to_column)
    other, _ = lax.optimization_barrier((other, both))
    source = join(own, other)
    source = join(source, send(source, lambda row, col: (row, col ^ S_MASKS[1])))
    receiver = join(
        receiver,
        send(receiver, lambda row, col: (row ^ (2 if row & 1 else 4), col)),
    )
    others = send(source, lambda row, col: (row, col ^ S_MASKS[2]))
    receiver = join(
        receiver,
        send(receiver, lambda row, col: (row ^ (4 if row & 1 else 2), col)),
    )
    rest = send(receiver, lambda row, col: (row ^ 1, col))
    return correlate(source, others, receiver, rest)


def solution(mesh):
    in_specs = (P(None, AXES, None), P(), P(), P(AXES))
    out_specs = P(None, "row", "col")
    return jax.shard_map(body, mesh=mesh, in_specs=in_specs, out_specs=out_specs, check_vma=False)
```

profile of v0, /device:TPU:22, one launch (start us, length us, event | category | flops | bytes accessed | tf_op | source)
XLA Modules:
  0.0 29.3 jit_solution(8675247264769085540)
XLA Ops:
  0.0 2.4 %whiten.1 = bf16[16,512]{1,0:T(8,128)(2,1)S(1)} custom-call(s32[6]{0:T(128)} %plan_ref.1, bf16[6,16,2560]{2,1,0:T(8,128)(2,1)} %record_ref.1, f32[200]{0:T(256)} %taps_ref.1, s32[16]{0:T(128)} %quality_ref.1), custom_call_target="tpu_custom_call" | custom-call | flops 268435456 | bytes 524288 | tf_op jit(solution)/shard_map/whiten/pallas_call | solution.py:99
  2.4 0.1 collective-permute-start.1
  2.5 4.0 %collective-permute-start = (bf16[16,512]{1,0:T(8,128)(2,1)S(1)}, bf16[16,512]{1,0:T(8,128)(2,1)S(1)}, u32[]{:S(2)}, u32[]{:S(2)}) collective-permute-start(bf16[16,512]{1,0:T(8,128)(2,1)S(1)} %whiten.1), channel_id=1, source_target_pairs={{0,1},{1,0},{2,3},{3,2},{4,5},{5,4},{6,7},{7,6},{8,9},{9,8},{10,11... | collective-permute-start | bytes 49160 | tf_op jit(solution)/shard_map/ppermute | solution.py:214
  6.4 0.0 collective-permute-done.1
  6.5 0.7 %collective-permute-start.4 = (bf16[32,512]{1,0:T(8,128)(2,1)S(1)}, bf16[32,512]{1,0:T(8,128)(2,1)S(1)}, u32[]{:S(2)}, u32[]{:S(2)}) collective-permute-start(bf16[32,512]{1,0:T(8,128)(2,1)S(1)} %pad_maximum_fusion.3), channel_id=1, source_target_pairs={{0,64},{1,80},{2,96},{3,112},{4,0},{5,16},{6,32},{7,48},{8,40},{9,... | collective-permute-start | bytes 98312 | tf_op jit(solution)/shard_map/ppermute | solution.py:214
  7.2 1.0 %collective-permute-done = bf16[16,512]{1,0:T(8,128)(2,1)S(1)} collective-permute-done((bf16[16,512]{1,0:T(8,128)(2,1)S(1)}, bf16[16,512]{1,0:T(8,128)(2,1)S(1)}, u32[]{:S(2)}, u32[]{:S(2)}) %collective-permute-start) | collective-permute-done | bytes 16416 | tf_op jit(solution)/shard_map/ppermute | solution.py:214
  8.2 1.9 %collective-permute-start.2 = (bf16[32,512]{1,0:T(8,128)(2,1)S(1)}, bf16[32,512]{1,0:T(8,128)(2,1)S(1)}, u32[]{:S(2)}, u32[]{:S(2)}) collective-permute-start(bf16[32,512]{1,0:T(8,128)(2,1)S(1)} %pad_maximum_fusion.2), channel_id=1, source_target_pairs={{0,4},{1,5},{2,6},{3,7},{4,0},{5,1},{6,2},{7,3},{8,12},{9,13},{10,... | collective-permute-start | bytes 98312 | tf_op jit(solution)/shard_map/ppermute | solution.py:214
  10.1 3.1 %collective-permute-done.4 = bf16[32,512]{1,0:T(8,128)(2,1)S(1)} collective-permute-done((bf16[32,512]{1,0:T(8,128)(2,1)S(1)}, bf16[32,512]{1,0:T(8,128)(2,1)S(1)}, u32[]{:S(2)}, u32[]{:S(2)}) %collective-permute-start.4) | collective-permute-done | bytes 32800 | tf_op jit(solution)/shard_map/ppermute | solution.py:214
  13.2 0.1 collective-permute-start.5
  13.3 3.8 %collective-permute-done.5 = bf16[32,512]{1,0:T(8,128)(2,1)S(1)} collective-permute-done((bf16[32,512]{1,0:T(8,128)(2,1)S(1)}, bf16[32,512]{1,0:T(8,128)(2,1)S(1)}, u32[]{:S(2)}, u32[]{:S(2)}) %collective-permute-start.5) | collective-permute-done | bytes 32800 | tf_op jit(solution)/shard_map/ppermute | solution.py:214
  17.1 1.6 %collective-permute-start.6 = (bf16[64,512]{1,0:T(8,128)(2,1)S(1)}, bf16[64,512]{1,0:T(8,128)(2,1)S(1)}, u32[]{:S(2)}, u32[]{:S(2)}) collective-permute-start(bf16[64,512]{1,0:T(8,128)(2,1)S(1)} %pad_maximum_fusion.1), channel_id=1, source_target_pairs={{0,16},{1,17},{2,18},{3,19},{4,20},{5,21},{6,22},{7,23},{8,40},{9,... | collective-permute-start | bytes 196616 | tf_op jit(solution)/shard_map/ppermute | solution.py:214
  18.7 2.7 %collective-permute-done.6 = bf16[64,512]{1,0:T(8,128)(2,1)S(1)} collective-permute-done((bf16[64,512]{1,0:T(8,128)(2,1)S(1)}, bf16[64,512]{1,0:T(8,128)(2,1)S(1)}, u32[]{:S(2)}, u32[]{:S(2)}) %collective-permute-start.6) | collective-permute-done | bytes 65568 | tf_op jit(solution)/shard_map/ppermute | solution.py:214
  21.4 0.0 collective-permute-start.7
  21.4 0.0 collective-permute-done.2
  21.4 0.1 collective-permute-start.3
  21.5 4.5 %collective-permute-done.3.s1_ref = bf16[64,512]{1,0:T(8,128)(2,1)S(1)} collective-permute-done((bf16[64,512]{1,0:T(8,128)(2,1)S(1)}, bf16[64,512]{1,0:T(8,128)(2,1)S(1)}, u32[]{:S(2)}, u32[]{:S(2)}) %collective-permute-start.3) | collective-permute-done | bytes 65568 | tf_op jit(solution)/shard_map/ppermute | solution.py:214
  26.0 0.0 collective-permute-done.7.r1_ref
  26.0 3.3 %correlate.1 = f32[51,128,256]{2,1,0:T(8,128)} custom-call(bf16[64,512]{1,0:T(8,128)(2,1)S(1)} %pad_maximum_fusion.s0_ref, bf16[64,512]{1,0:T(8,128)(2,1)S(1)} %collective-permute-done.3.s1_ref, bf16[128,512]{1,0:T(8,128)(2,1)S(1)} %constant_dynamic-update-slice_fusion.r0_ref, bf16[128,512]{1,0:T(8,128)(2,1)S(1)} %collective-permute-done.7.r1_ref), custom_call_target="tpu_custom_call" | custom-call | flops 2147483648 | bytes 8388608 | tf_op jit(solution)/shard_map/correlate/pallas_call | solution.py:191
  (7 shorter events, 0.0 us)
Async XLA Ops:
  2.4 4.1 %collective-permute-start.1 = (bf16[16,512]{1,0:T(8,128)(2,1)S(1)}, bf16[16,512]{1,0:T(8,128)(2,1)S(1)}, u32[]{:S(2)}, u32[]{:S(2)}) collective-permute-start(bf16[16,512]{1,0:T(8,128)(2,1)S(1)} %whiten.1), channel_id=1, source_target_pairs={{0,8},{1,9},{2,10},{3,11},{4,12},{5,13},{6,14},{7,15},{8,0},{9,1},... | collective-permute-start | bytes 49160 | tf_op jit(solution)/shard_map/ppermute | solution.py:214
  2.5 5.7 %collective-permute-start = (bf16[16,512]{1,0:T(8,128)(2,1)S(1)}, bf16[16,512]{1,0:T(8,128)(2,1)S(1)}, u32[]{:S(2)}, u32[]{:S(2)}) collective-permute-start(bf16[16,512]{1,0:T(8,128)(2,1)S(1)} %whiten.1), channel_id=1, source_target_pairs={{0,1},{1,0},{2,3},{3,2},{4,5},{5,4},{6,7},{7,6},{8,9},{9,8},{10,11... | collective-permute-start | bytes 49160 | tf_op jit(solution)/shard_map/ppermute | solution.py:214
  6.5 6.7 %collective-permute-start.4 = (bf16[32,512]{1,0:T(8,128)(2,1)S(1)}, bf16[32,512]{1,0:T(8,128)(2,1)S(1)}, u32[]{:S(2)}, u32[]{:S(2)}) collective-permute-start(bf16[32,512]{1,0:T(8,128)(2,1)S(1)} %pad_maximum_fusion.3), channel_id=1, source_target_pairs={{0,64},{1,80},{2,96},{3,112},{4,0},{5,16},{6,32},{7,48},{8,40},{9,... | collective-permute-start | bytes 98312 | tf_op jit(solution)/shard_map/ppermute | solution.py:214
  8.2 13.2 %collective-permute-start.2 = (bf16[32,512]{1,0:T(8,128)(2,1)S(1)}, bf16[32,512]{1,0:T(8,128)(2,1)S(1)}, u32[]{:S(2)}, u32[]{:S(2)}) collective-permute-start(bf16[32,512]{1,0:T(8,128)(2,1)S(1)} %pad_maximum_fusion.2), channel_id=1, source_target_pairs={{0,4},{1,5},{2,6},{3,7},{4,0},{5,1},{6,2},{7,3},{8,12},{9,13},{10,... | collective-permute-start | bytes 98312 | tf_op jit(solution)/shard_map/ppermute | solution.py:214
  13.2 3.9 %collective-permute-start.5 = (bf16[32,512]{1,0:T(8,128)(2,1)S(1)}, bf16[32,512]{1,0:T(8,128)(2,1)S(1)}, u32[]{:S(2)}, u32[]{:S(2)}) collective-permute-start(bf16[32,512]{1,0:T(8,128)(2,1)S(1)} %collective-permute-done.4), channel_id=1, source_target_pairs={{0,32},{1,33},{2,34},{3,35},{4,36},{5,37},{6,38},{7,39},{8,24},{9,... | collective-permute-start | bytes 98312 | tf_op jit(solution)/shard_map/ppermute | solution.py:214
  17.1 4.3 %collective-permute-start.6 = (bf16[64,512]{1,0:T(8,128)(2,1)S(1)}, bf16[64,512]{1,0:T(8,128)(2,1)S(1)}, u32[]{:S(2)}, u32[]{:S(2)}) collective-permute-start(bf16[64,512]{1,0:T(8,128)(2,1)S(1)} %pad_maximum_fusion.1), channel_id=1, source_target_pairs={{0,16},{1,17},{2,18},{3,19},{4,20},{5,21},{6,22},{7,23},{8,40},{9,... | collective-permute-start | bytes 196616 | tf_op jit(solution)/shard_map/ppermute | solution.py:214
  21.4 4.6 %collective-permute-start.7 = (bf16[128,512]{1,0:T(8,128)(2,1)S(1)}, bf16[128,512]{1,0:T(8,128)(2,1)S(1)}, u32[]{:S(2)}, u32[]{:S(2)}) collective-permute-start(bf16[128,512]{1,0:T(8,128)(2,1)S(1)} %constant_dynamic-update-slice_fusion.r0_ref), channel_id=1, source_target_pairs={{0,8},{1,9},{2,10},{3,11},{4,12},{5,13},{6,14},{7,15},{8,0},{9,1},... | collective-permute-start | bytes 393224 | tf_op jit(solution)/shard_map/ppermute | solution.py:214
  21.4 4.6 %collective-permute-start.3 = (bf16[64,512]{1,0:T(8,128)(2,1)S(1)}, bf16[64,512]{1,0:T(8,128)(2,1)S(1)}, u32[]{:S(2)}, u32[]{:S(2)}) collective-permute-start(bf16[64,512]{1,0:T(8,128)(2,1)S(1)} %pad_maximum_fusion.s0_ref), channel_id=1, source_target_pairs={{0,2},{1,3},{2,0},{3,1},{4,6},{5,7},{6,4},{7,5},{8,10},{9,11},{10,... | collective-permute-start | bytes 196616 | tf_op jit(solution)/shard_map/ppermute | solution.py:214
where the time goes:
time: 29.5 us; the launch traced here: 29.3 us
  waiting for transfers between devices  15.1 us (51%)
  starting transfers between devices  8.44 us (29%)
  Pallas kernels  5.73 us (19%)
    ppermute x8, waiting for transfers between devices, send(): return lax.ppermute(block, AXES, pairs)  15.1 us
    ppermute x8, starting transfers between devices, send(): return lax.ppermute(block, AXES, pairs)  8.44 us
    pallas_call x1, Pallas kernels, correlate(): pl.pallas_call(correlate_kernel, name='correlate', out_shape=jax.ShapeDty...  3.35 us
    pallas_call x1, Pallas kernels, whiten(): pl.pallas_call(whiten_kernel, name='whiten', out_shape=jax.ShapeDtypeStru...  2.39 us
  transfers between devices with their start and end apart: 8, of which 5 were waited for; matrix products, arithmetic and copies ran while one was open for 0% of the time, Pallas kernels for 0%

commit v1 on v0

--- a/solution.py
+++ b/solution.py
@@ -116,7 +116,7 @@
     )(*(pltpu.with_memory_space_constraint(v, pltpu.HBM) for v in (plan, record, taps, quality)))
 
 
-S_MASKS = (1, 4, 2)
+S_MASKS = (0, 2, 4, 6)
 
 
 def spread(index, *masks):
@@ -127,16 +127,21 @@
     return place
 
 
-def correlate_kernel(s0_ref, s1_ref, r0_ref, r1_ref, out_ref, source, receiver, products, sems):
+def correlate_kernel(*refs):
+    s_refs, (r0_ref, r1_ref), (out_ref, source, receiver, products, sems) = (
+        refs[:4],
+        refs[4:6],
+        refs[6:],
+    )
     count, length = source.shape
     chans = count // 8
     col, row = lax.axis_index("col"), lax.axis_index("row")
-    for t in range(8):
-        place = col ^ spread(t, *S_MASKS)
-        part = (s0_ref, s1_ref)[t // 4]
-        source[pl.ds(pl.multiple_of(place * chans, chans), chans)] = part[
-            t % 4 * chans : (t % 4 + 1) * chans
-        ].astype(jnp.float32)
+    for part, mask in zip(s_refs, S_MASKS):
+        for j in range(2):
+            start = (col ^ mask ^ j) * chans
+            source[pl.ds(pl.multiple_of(start, chans), chans)] = part[
+                j * chans : (j + 1) * chans
+            ].astype(jnp.float32)
     for half in range(2):
         core = (row & 1) ^ half
         part = (r0_ref, r1_ref)[half]
@@ -185,14 +190,14 @@
 
 
 def correlate(*parts):
-    count, width = 2 * parts[0].shape[0], 2 * parts[2].shape[0]
+    count, width = 4 * parts[0].shape[0], 2 * parts[4].shape[0]
     length = parts[0].shape[1]
     whole = pl.BlockSpec(memory_space=pltpu.VMEM)
     return pl.pallas_call(
         correlate_kernel,
         name="correlate",
         out_shape=jax.ShapeDtypeStruct((LAGS, count, width), jnp.float32),
-        in_specs=[whole] * 4,
+        in_specs=[whole] * 6,
         out_specs=pl.BlockSpec(memory_space=pl.ANY),
         scratch_shapes=[
             pltpu.VMEM((count, length), jnp.float32),
@@ -227,22 +232,22 @@
 def body(record, taps, plan, quality):
     own = whiten(record, taps, plan, quality)
     both = join(own, send(own, lambda row, col: (row ^ 1, col)))
-    other = send(own, lambda row, col: (row, col ^ S_MASKS[0]))
+    other = send(own, lambda row, col: (row, col ^ 1))
     receiver = send(both, to_column)
     other, _ = lax.optimization_barrier((other, both))
-    source = join(own, other)
-    source = join(source, send(source, lambda row, col: (row, col ^ S_MASKS[1])))
+    sources = [join(own, other)]
+    for mask in S_MASKS[1:]:
+        sources.append(send(sources[0], lambda row, col: (row, col ^ mask)))
     receiver = join(
         receiver,
         send(receiver, lambda row, col: (row ^ (2 if row & 1 else 4), col)),
     )
-    others = send(source, lambda row, col: (row, col ^ S_MASKS[2]))
     receiver = join(
         receiver,
         send(receiver, lambda row, col: (row ^ (4 if row & 1 else 2), col)),
     )
     rest = send(receiver, lambda row, col: (row ^ 1, col))
-    return correlate(source, others, receiver, rest)
+    return correlate(*sources, receiver, rest)
 
 
 def solution(mesh):

time: 29.5 us -> 32.7 us (1.11)
  the two profiles are of different devices: /device:TPU:22 before, /device:TPU:1 now
where the time goes in v1:
time: 32.7 us; the launch traced here: 32.6 us
  starting transfers between devices  18.8 us (57%)
  waiting for transfers between devices  7.97 us (24%)
  Pallas kernels  5.74 us (18%)
    ppermute x9, starting transfers between devices, send(): return lax.ppermute(block, AXES, pairs)  18.8 us
    ppermute x9, waiting for transfers between devices, send(): return lax.ppermute(block, AXES, pairs)  7.97 us
    pallas_call x1, Pallas kernels, correlate(): pl.pallas_call(correlate_kernel, name='correlate', out_shape=jax.ShapeDty...  3.35 us
    pallas_call x1, Pallas kernels, whiten(): pl.pallas_call(whiten_kernel, name='whiten', out_shape=jax.ShapeDtypeStru...  2.38 us
  transfers between devices with their start and end apart: 9, of which 7 were waited for; matrix products, arithmetic and copies ran while one was open for 0% of the time, Pallas kernels for 0%

profile of v1, /device:TPU:1, one launch (start us, length us, event | category | flops | bytes accessed | tf_op | source)
XLA Modules:
  0.0 32.6 jit_solution(9062050128713884594)
XLA Ops:
  0.0 2.4 %whiten.1 = bf16[16,512]{1,0:T(8,128)(2,1)S(1)} custom-call(s32[6]{0:T(128)} %plan_ref.1, bf16[6,16,2560]{2,1,0:T(8,128)(2,1)} %record_ref.1, f32[200]{0:T(256)} %taps_ref.1, s32[16]{0:T(128)} %quality_ref.1), custom_call_target="tpu_custom_call" | custom-call | flops 268435456 | bytes 524288 | tf_op jit(solution)/shard_map/whiten/pallas_call | solution.py:99
  2.4 1.5 %collective-permute-start.1 = (bf16[16,512]{1,0:T(8,128)(2,1)S(1)}, bf16[16,512]{1,0:T(8,128)(2,1)S(1)}, u32[]{:S(2)}, u32[]{:S(2)}) collective-permute-start(bf16[16,512]{1,0:T(8,128)(2,1)S(1)} %whiten.1), channel_id=1, source_target_pairs={{0,8},{1,9},{2,10},{3,11},{4,12},{5,13},{6,14},{7,15},{8,0},{9,1},... | collective-permute-start | bytes 49160 | tf_op jit(solution)/shard_map/ppermute | solution.py:219
  3.9 0.8 %collective-permute-done.1 = bf16[16,512]{1,0:T(8,128)(2,1)S(1)} collective-permute-done((bf16[16,512]{1,0:T(8,128)(2,1)S(1)}, bf16[16,512]{1,0:T(8,128)(2,1)S(1)}, u32[]{:S(2)}, u32[]{:S(2)}) %collective-permute-start.1) | collective-permute-done | bytes 16416 | tf_op jit(solution)/shard_map/ppermute | solution.py:219
  4.7 1.4 %collective-permute-start.5 = (bf16[32,512]{1,0:T(8,128)(2,1)S(1)}, bf16[32,512]{1,0:T(8,128)(2,1)S(1)}, u32[]{:S(2)}, u32[]{:S(2)}) collective-permute-start(bf16[32,512]{1,0:T(8,128)(2,1)S(1)} %pad_maximum_fusion.1), channel_id=1, source_target_pairs={{0,64},{1,80},{2,96},{3,112},{4,0},{5,16},{6,32},{7,48},{8,40},{9,... | collective-permute-start | bytes 98312 | tf_op jit(solution)/shard_map/ppermute | solution.py:219
  6.1 3.2 %collective-permute-start = (bf16[16,512]{1,0:T(8,128)(2,1)S(1)}, bf16[16,512]{1,0:T(8,128)(2,1)S(1)}, u32[]{:S(2)}, u32[]{:S(2)}) collective-permute-start(bf16[16,512]{1,0:T(8,128)(2,1)S(1)} %whiten.1), channel_id=1, source_target_pairs={{0,1},{1,0},{2,3},{3,2},{4,5},{5,4},{6,7},{7,6},{8,9},{9,8},{10,11... | collective-permute-start | bytes 49160 | tf_op jit(solution)/shard_map/ppermute | solution.py:219
  9.3 1.1 %collective-permute-done = bf16[16,512]{1,0:T(8,128)(2,1)S(1)} collective-permute-done((bf16[16,512]{1,0:T(8,128)(2,1)S(1)}, bf16[16,512]{1,0:T(8,128)(2,1)S(1)}, u32[]{:S(2)}, u32[]{:S(2)}) %collective-permute-start) | collective-permute-done | bytes 16416 | tf_op jit(solution)/shard_map/ppermute | solution.py:219
  10.4 0.0 collective-permute-done.5
  10.4 2.8 %collective-permute-start.6 = (bf16[32,512]{1,0:T(8,128)(2,1)S(1)}, bf16[32,512]{1,0:T(8,128)(2,1)S(1)}, u32[]{:S(2)}, u32[]{:S(2)}) collective-permute-start(bf16[32,512]{1,0:T(8,128)(2,1)S(1)} %collective-permute-done.5), channel_id=1, source_target_pairs={{0,32},{1,33},{2,34},{3,35},{4,36},{5,37},{6,38},{7,39},{8,24},{9,... | collective-permute-start | bytes 98312 | tf_op jit(solution)/shard_map/ppermute | solution.py:219
  13.2 1.4 %collective-permute-done.6 = bf16[32,512]{1,0:T(8,128)(2,1)S(1)} collective-permute-done((bf16[32,512]{1,0:T(8,128)(2,1)S(1)}, bf16[32,512]{1,0:T(8,128)(2,1)S(1)}, u32[]{:S(2)}, u32[]{:S(2)}) %collective-permute-start.6) | collective-permute-done | bytes 32800 | tf_op jit(solution)/shard_map/ppermute | solution.py:219
  14.6 1.3 %collective-permute-start.7 = (bf16[64,512]{1,0:T(8,128)(2,1)S(1)}, bf16[64,512]{1,0:T(8,128)(2,1)S(1)}, u32[]{:S(2)}, u32[]{:S(2)}) collective-permute-start(bf16[64,512]{1,0:T(8,128)(2,1)S(1)} %pad_maximum_fusion), channel_id=1, source_target_pairs={{0,16},{1,17},{2,18},{3,19},{4,20},{5,21},{6,22},{7,23},{8,40},{9,... | collective-permute-start | bytes 196616 | tf_op jit(solution)/shard_map/ppermute | solution.py:219
  15.9 1.8 %collective-permute-done.7 = bf16[64,512]{1,0:T(8,128)(2,1)S(1)} collective-permute-done((bf16[64,512]{1,0:T(8,128)(2,1)S(1)}, bf16[64,512]{1,0:T(8,128)(2,1)S(1)}, u32[]{:S(2)}, u32[]{:S(2)}) %collective-permute-start.7) | collective-permute-done | bytes 65568 | tf_op jit(solution)/shard_map/ppermute | solution.py:219
  17.7 5.4 %collective-permute-start.8 = (bf16[128,512]{1,0:T(8,128)(2,1)S(1)}, bf16[128,512]{1,0:T(8,128)(2,1)S(1)}, u32[]{:S(2)}, u32[]{:S(2)}) collective-permute-start(bf16[128,512]{1,0:T(8,128)(2,1)S(1)} %constant_dynamic-update-slice_fusion.refs_4_), channel_id=1, source_target_pairs={{0,8},{1,9},{2,10},{3,11},{4,12},{5,13},{6,14},{7,15},{8,0},{9,1},... | collective-permute-start | bytes 393224 | tf_op jit(solution)/shard_map/ppermute | solution.py:219
  23.2 0.7 %collective-permute-start.4 = (bf16[32,512]{1,0:T(8,128)(2,1)S(1)}, bf16[32,512]{1,0:T(8,128)(2,1)S(1)}, u32[]{:S(2)}, u32[]{:S(2)}) collective-permute-start(bf16[32,512]{1,0:T(8,128)(2,1)S(1)} %pad_maximum_fusion.2.refs_0_), channel_id=1, source_target_pairs={{0,6},{1,7},{2,4},{3,5},{4,2},{5,3},{6,0},{7,1},{8,14},{9,15},{10,... | collective-permute-start | bytes 98312 | tf_op jit(solution)/shard_map/ppermute | solution.py:219
  23.8 2.0 %collective-permute-start.3 = (bf16[32,512]{1,0:T(8,128)(2,1)S(1)}, bf16[32,512]{1,0:T(8,128)(2,1)S(1)}, u32[]{:S(2)}, u32[]{:S(2)}) collective-permute-start(bf16[32,512]{1,0:T(8,128)(2,1)S(1)} %pad_maximum_fusion.2.refs_0_), channel_id=1, source_target_pairs={{0,4},{1,5},{2,6},{3,7},{4,0},{5,1},{6,2},{7,3},{8,12},{9,13},{10,... | collective-permute-start | bytes 98312 | tf_op jit(solution)/shard_map/ppermute | solution.py:219
  25.8 0.6 %collective-permute-start.2 = (bf16[32,512]{1,0:T(8,128)(2,1)S(1)}, bf16[32,512]{1,0:T(8,128)(2,1)S(1)}, u32[]{:S(2)}, u32[]{:S(2)}) collective-permute-start(bf16[32,512]{1,0:T(8,128)(2,1)S(1)} %pad_maximum_fusion.2.refs_0_), channel_id=1, source_target_pairs={{0,2},{1,3},{2,0},{3,1},{4,6},{5,7},{6,4},{7,5},{8,10},{9,11},{10,... | collective-permute-start | bytes 98312 | tf_op jit(solution)/shard_map/ppermute | solution.py:219
  26.4 0.7 %collective-permute-done.4.refs_3_ = bf16[32,512]{1,0:T(8,128)(2,1)S(1)} collective-permute-done((bf16[32,512]{1,0:T(8,128)(2,1)S(1)}, bf16[32,512]{1,0:T(8,128)(2,1)S(1)}, u32[]{:S(2)}, u32[]{:S(2)}) %collective-permute-start.4) | collective-permute-done | bytes 32800 | tf_op jit(solution)/shard_map/ppermute | solution.py:219
  27.1 0.9 %collective-permute-done.3.refs_2_ = bf16[32,512]{1,0:T(8,128)(2,1)S(1)} collective-permute-done((bf16[32,512]{1,0:T(8,128)(2,1)S(1)}, bf16[32,512]{1,0:T(8,128)(2,1)S(1)}, u32[]{:S(2)}, u32[]{:S(2)}) %collective-permute-start.3) | collective-permute-done | bytes 32800 | tf_op jit(solution)/shard_map/ppermute | solution.py:219
  28.1 1.1 %collective-permute-done.2.refs_1_ = bf16[32,512]{1,0:T(8,128)(2,1)S(1)} collective-permute-done((bf16[32,512]{1,0:T(8,128)(2,1)S(1)}, bf16[32,512]{1,0:T(8,128)(2,1)S(1)}, u32[]{:S(2)}, u32[]{:S(2)}) %collective-permute-start.2) | collective-permute-done | bytes 32800 | tf_op jit(solution)/shard_map/ppermute | solution.py:219
  29.2 0.0 collective-permute-done.8.refs_5_
  29.2 3.4 %correlate.1 = f32[51,128,256]{2,1,0:T(8,128)} custom-call(bf16[32,512]{1,0:T(8,128)(2,1)S(1)} %pad_maximum_fusion.2.refs_0_, bf16[32,512]{1,0:T(8,128)(2,1)S(1)} %collective-permute-done.2.refs_1_, bf16[32,512]{1,0:T(8,128)(2,1)S(1)} %collective-permute-done.3.refs_2_, bf16[32,512]{1,0:T(8,128)(2,1)S(1)} %collective-permute-done.4.refs_3_, ...), custom_call_target="tpu_custom_call" | custom-call | flops 2147483648 | bytes 8388608 | tf_op jit(solution)/shard_map/correlate/pallas_call | solution.py:196
  (6 shorter events, 0.0 us)
Async XLA Ops:
  2.4 2.3 %collective-permute-start.1 = (bf16[16,512]{1,0:T(8,128)(2,1)S(1)}, bf16[16,512]{1,0:T(8,128)(2,1)S(1)}, u32[]{:S(2)}, u32[]{:S(2)}) collective-permute-start(bf16[16,512]{1,0:T(8,128)(2,1)S(1)} %whiten.1), channel_id=1, source_target_pairs={{0,8},{1,9},{2,10},{3,11},{4,12},{5,13},{6,14},{7,15},{8,0},{9,1},... | collective-permute-start | bytes 49160 | tf_op jit(solution)/shard_map/ppermute | solution.py:219
  4.7 5.7 %collective-permute-start.5 = (bf16[32,512]{1,0:T(8,128)(2,1)S(1)}, bf16[32,512]{1,0:T(8,128)(2,1)S(1)}, u32[]{:S(2)}, u32[]{:S(2)}) collective-permute-start(bf16[32,512]{1,0:T(8,128)(2,1)S(1)} %pad_maximum_fusion.1), channel_id=1, source_target_pairs={{0,64},{1,80},{2,96},{3,112},{4,0},{5,16},{6,32},{7,48},{8,40},{9,... | collective-permute-start | bytes 98312 | tf_op jit(solution)/shard_map/ppermute | solution.py:219
  6.1 4.3 %collective-permute-start = (bf16[16,512]{1,0:T(8,128)(2,1)S(1)}, bf16[16,512]{1,0:T(8,128)(2,1)S(1)}, u32[]{:S(2)}, u32[]{:S(2)}) collective-permute-start(bf16[16,512]{1,0:T(8,128)(2,1)S(1)} %whiten.1), channel_id=1, source_target_pairs={{0,1},{1,0},{2,3},{3,2},{4,5},{5,4},{6,7},{7,6},{8,9},{9,8},{10,11... | collective-permute-start | bytes 49160 | tf_op jit(solution)/shard_map/ppermute | solution.py:219
  10.4 4.2 %collective-permute-start.6 = (bf16[32,512]{1,0:T(8,128)(2,1)S(1)}, bf16[32,512]{1,0:T(8,128)(2,1)S(1)}, u32[]{:S(2)}, u32[]{:S(2)}) collective-permute-start(bf16[32,512]{1,0:T(8,128)(2,1)S(1)} %collective-permute-done.5), channel_id=1, source_target_pairs={{0,32},{1,33},{2,34},{3,35},{4,36},{5,37},{6,38},{7,39},{8,24},{9,... | collective-permute-start | bytes 98312 | tf_op jit(solution)/shard_map/ppermute | solution.py:219
  14.6 3.1 %collective-permute-start.7 = (bf16[64,512]{1,0:T(8,128)(2,1)S(1)}, bf16[64,512]{1,0:T(8,128)(2,1)S(1)}, u32[]{:S(2)}, u32[]{:S(2)}) collective-permute-start(bf16[64,512]{1,0:T(8,128)(2,1)S(1)} %pad_maximum_fusion), channel_id=1, source_target_pairs={{0,16},{1,17},{2,18},{3,19},{4,20},{5,21},{6,22},{7,23},{8,40},{9,... | collective-permute-start | bytes 196616 | tf_op jit(solution)/shard_map/ppermute | solution.py:219
  17.7 11.5 %collective-permute-start.8 = (bf16[128,512]{1,0:T(8,128)(2,1)S(1)}, bf16[128,512]{1,0:T(8,128)(2,1)S(1)}, u32[]{:S(2)}, u32[]{:S(2)}) collective-permute-start(bf16[128,512]{1,0:T(8,128)(2,1)S(1)} %constant_dynamic-update-slice_fusion.refs_4_), channel_id=1, source_target_pairs={{0,8},{1,9},{2,10},{3,11},{4,12},{5,13},{6,14},{7,15},{8,0},{9,1},... | collective-permute-start | bytes 393224 | tf_op jit(solution)/shard_map/ppermute | solution.py:219
  23.2 4.0 %collective-permute-start.4 = (bf16[32,512]{1,0:T(8,128)(2,1)S(1)}, bf16[32,512]{1,0:T(8,128)(2,1)S(1)}, u32[]{:S(2)}, u32[]{:S(2)}) collective-permute-start(bf16[32,512]{1,0:T(8,128)(2,1)S(1)} %pad_maximum_fusion.2.refs_0_), channel_id=1, source_target_pairs={{0,6},{1,7},{2,4},{3,5},{4,2},{5,3},{6,0},{7,1},{8,14},{9,15},{10,... | collective-permute-start | bytes 98312 | tf_op jit(solution)/shard_map/ppermute | solution.py:219
  23.8 4.3 %collective-permute-start.3 = (bf16[32,512]{1,0:T(8,128)(2,1)S(1)}, bf16[32,512]{1,0:T(8,128)(2,1)S(1)}, u32[]{:S(2)}, u32[]{:S(2)}) collective-permute-start(bf16[32,512]{1,0:T(8,128)(2,1)S(1)} %pad_maximum_fusion.2.refs_0_), channel_id=1, source_target_pairs={{0,4},{1,5},{2,6},{3,7},{4,0},{5,1},{6,2},{7,3},{8,12},{9,13},{10,... | collective-permute-start | bytes 98312 | tf_op jit(solution)/shard_map/ppermute | solution.py:219
  25.8 3.4 %collective-permute-start.2 = (bf16[32,512]{1,0:T(8,128)(2,1)S(1)}, bf16[32,512]{1,0:T(8,128)(2,1)S(1)}, u32[]{:S(2)}, u32[]{:S(2)}) collective-permute-start(bf16[32,512]{1,0:T(8,128)(2,1)S(1)} %pad_maximum_fusion.2.refs_0_), channel_id=1, source_target_pairs={{0,2},{1,3},{2,0},{3,1},{4,6},{5,7},{6,4},{7,5},{8,10},{9,11},{10,... | collective-permute-start | bytes 98312 | tf_op jit(solution)/shard_map/ppermute | solution.py:219

commit v2 on v1

--- a/solution.py
+++ b/solution.py
@@ -21,19 +21,24 @@
 GROUP = 3
 
 
-def whiten_kernel(plan_ref, record_ref, taps_ref, quality_ref, out_ref, samples, sems):
+def whiten_kernel(
+    plan_hbm, record_hbm, taps_hbm, quality_hbm, out_ref, plan, samples, taps_ref, quality_ref, sems
+):
     chans = out_ref.shape[0]
     f32, bf16 = jnp.float32, jnp.bfloat16
-    raw = record_ref.shape[2]
-
-    def copy(s):
-        return pltpu.make_async_copy(
-            record_ref.at[plan_ref[s]], samples.at[s, :, pl.ds(0, raw)], sems.at[s]
-        )
-
-    for s in range(SUB):
-        copy(s).start()
-    samples[:, :, raw:] = jnp.zeros((SUB, chans, samples.shape[2] - raw), bf16)
+    slots, _, raw = record_hbm.shape
+    copies = [
+        pltpu.make_async_copy(plan_hbm, plan, sems.at[0]),
+        pltpu.make_async_copy(taps_hbm, taps_ref, sems.at[1]),
+        pltpu.make_async_copy(quality_hbm, quality_ref, sems.at[2]),
+    ] + [
+        pltpu.make_async_copy(record_hbm.at[s], samples.at[s, :, pl.ds(0, raw)], sems.at[3 + s])
+        for s in range(slots)
+    ]
+    for copy in copies:
+        copy.start()
+    samples[:, :, raw:] = jnp.zeros((slots, chans, samples.shape[2] - raw), bf16)
+    copies[1].wait()
     taps = taps_ref[...].reshape(1, TAPS)
     table = jnp.broadcast_to(
         jnp.concatenate([taps, jnp.zeros((1, SPAN - TAPS), f32)], axis=1), (32, SPAN)
@@ -50,16 +55,17 @@
     band = jnp.where(jnp.abs(i - j) <= HALFWIN, 1.0, 0.0).astype(bf16)
     a = lax.broadcasted_iota(jnp.int32, (chans, chans), 0)
     b = lax.broadcasted_iota(jnp.int32, (chans, chans), 1)
+    copies[2].wait()
     across = jnp.broadcast_to(
         quality_ref[...].reshape(1, chans).astype(f32), (chans, chans)
     )
     quality = jnp.sum(jnp.where(a == b, across, 0.0), axis=1, keepdims=True)
-    for s in range(SUB):
-        copy(s).wait()
+    for copy in copies[:1] + copies[3:]:
+        copy.wait()
     both = lax.dot_general(
         jnp.concatenate(
             [
-                samples[s, :, b * SEGMENT : b * SEGMENT + SPAN]
+                samples[plan[s], :, b * SEGMENT : b * SEGMENT + SPAN]
                 for s in range(SUB)
                 for b in range(4)
             ],
@@ -100,16 +106,14 @@
         whiten_kernel,
         name="whiten",
         out_shape=jax.ShapeDtypeStruct((chans, SUB * FRAMES), jnp.bfloat16),
-        in_specs=[
-            pl.BlockSpec(memory_space=pltpu.SMEM),
-            pl.BlockSpec(memory_space=pltpu.HBM),
-            pl.BlockSpec(memory_space=pltpu.VMEM),
-            pl.BlockSpec(memory_space=pltpu.VMEM),
-        ],
+        in_specs=[pl.BlockSpec(memory_space=pltpu.HBM)] * 4,
         out_specs=pl.BlockSpec(memory_space=pltpu.VMEM),
         scratch_shapes=[
-            pltpu.VMEM((SUB, chans, raw + SPAN - SEGMENT), jnp.bfloat16),
-            pltpu.SemaphoreType.DMA((SUB,)),
+            pltpu.SMEM(plan.shape, jnp.int32),
+            pltpu.VMEM((record.shape[0], chans, raw + SPAN - SEGMENT), jnp.bfloat16),
+            pltpu.VMEM(taps.shape, jnp.float32),
+            pltpu.VMEM(quality.shape, jnp.int32),
+            pltpu.SemaphoreType.DMA((3 + record.shape[0],)),
         ],
         compiler_params=pltpu.CompilerParams(vmem_limit_bytes=8 << 20),
         cost_estimate=pl.CostEstimate(flops=1 << 28, bytes_accessed=1 << 19, transcendentals=0),

time: 32.7 us -> 32.1 us (0.982)
  Pallas kernels: 5.74 us -> 5.12 us
    pallas_call x1, Pallas kernels: 2.38 us -> 1.77 us  [whiten(): pl.pallas_call(whiten_kernel, name='whiten', out_shape=jax.ShapeDtypeStru...]
where the time goes in v2:
time: 32.1 us; the launch traced here: 31.9 us
  starting transfers between devices  18.8 us (59%)
  waiting for transfers between devices  7.97 us (25%)
  Pallas kernels  5.12 us (16%)
    ppermute x9, starting transfers between devices, send(): return lax.ppermute(block, AXES, pairs)  18.8 us
    ppermute x9, waiting for transfers between devices, send(): return lax.ppermute(block, AXES, pairs)  7.97 us
    pallas_call x1, Pallas kernels, correlate(): pl.pallas_call(correlate_kernel, name='correlate', out_shape=jax.ShapeDty...  3.35 us
    pallas_call x1, Pallas kernels, whiten(): pl.pallas_call(whiten_kernel, name='whiten', out_shape=jax.ShapeDtypeStru...  1.77 us
  transfers between devices with their start and end apart: 9, of which 7 were waited for; matrix products, arithmetic and copies ran while one was open for 0% of the time, Pallas kernels for 0%

profile of v2, /device:TPU:1, one launch (start us, length us, event | category | flops | bytes accessed | tf_op | source)
XLA Modules:
  0.0 31.9 jit_solution(6401757043922086509)
XLA Ops:
  0.0 1.8 %whiten.1 = bf16[16,512]{1,0:T(8,128)(2,1)S(1)} custom-call(s32[6]{0:T(128)} %plan_hbm.1, bf16[6,16,2560]{2,1,0:T(8,128)(2,1)} %record_hbm.1, f32[200]{0:T(256)} %taps_hbm.1, s32[16]{0:T(128)} %quality_hbm.1), custom_call_target="tpu_custom_call" | custom-call | flops 268435456 | bytes 524288 | tf_op jit(solution)/shard_map/whiten/pallas_call | solution.py:105
  1.8 1.5 %collective-permute-start.1 = (bf16[16,512]{1,0:T(8,128)(2,1)S(1)}, bf16[16,512]{1,0:T(8,128)(2,1)S(1)}, u32[]{:S(2)}, u32[]{:S(2)}) collective-permute-start(bf16[16,512]{1,0:T(8,128)(2,1)S(1)} %whiten.1), channel_id=1, source_target_pairs={{0,8},{1,9},{2,10},{3,11},{4,12},{5,13},{6,14},{7,15},{8,0},{9,1},... | collective-permute-start | bytes 49160 | tf_op jit(solution)/shard_map/ppermute | solution.py:223
  3.2 0.8 %collective-permute-done.1 = bf16[16,512]{1,0:T(8,128)(2,1)S(1)} collective-permute-done((bf16[16,512]{1,0:T(8,128)(2,1)S(1)}, bf16[16,512]{1,0:T(8,128)(2,1)S(1)}, u32[]{:S(2)}, u32[]{:S(2)}) %collective-permute-start.1) | collective-permute-done | bytes 16416 | tf_op jit(solution)/shard_map/ppermute | solution.py:223
  4.1 1.4 %collective-permute-start.5 = (bf16[32,512]{1,0:T(8,128)(2,1)S(1)}, bf16[32,512]{1,0:T(8,128)(2,1)S(1)}, u32[]{:S(2)}, u32[]{:S(2)}) collective-permute-start(bf16[32,512]{1,0:T(8,128)(2,1)S(1)} %pad_maximum_fusion.1), channel_id=1, source_target_pairs={{0,64},{1,80},{2,96},{3,112},{4,0},{5,16},{6,32},{7,48},{8,40},{9,... | collective-permute-start | bytes 98312 | tf_op jit(solution)/shard_map/ppermute | solution.py:223
  5.5 3.1 %collective-permute-start = (bf16[16,512]{1,0:T(8,128)(2,1)S(1)}, bf16[16,512]{1,0:T(8,128)(2,1)S(1)}, u32[]{:S(2)}, u32[]{:S(2)}) collective-permute-start(bf16[16,512]{1,0:T(8,128)(2,1)S(1)} %whiten.1), channel_id=1, source_target_pairs={{0,1},{1,0},{2,3},{3,2},{4,5},{5,4},{6,7},{7,6},{8,9},{9,8},{10,11... | collective-permute-start | bytes 49160 | tf_op jit(solution)/shard_map/ppermute | solution.py:223
  8.6 1.1 %collective-permute-done = bf16[16,512]{1,0:T(8,128)(2,1)S(1)} collective-permute-done((bf16[16,512]{1,0:T(8,128)(2,1)S(1)}, bf16[16,512]{1,0:T(8,128)(2,1)S(1)}, u32[]{:S(2)}, u32[]{:S(2)}) %collective-permute-start) | collective-permute-done | bytes 16416 | tf_op jit(solution)/shard_map/ppermute | solution.py:223
  9.8 0.0 collective-permute-done.5
  9.8 2.8 %collective-permute-start.6 = (bf16[32,512]{1,0:T(8,128)(2,1)S(1)}, bf16[32,512]{1,0:T(8,128)(2,1)S(1)}, u32[]{:S(2)}, u32[]{:S(2)}) collective-permute-start(bf16[32,512]{1,0:T(8,128)(2,1)S(1)} %collective-permute-done.5), channel_id=1, source_target_pairs={{0,32},{1,33},{2,34},{3,35},{4,36},{5,37},{6,38},{7,39},{8,24},{9,... | collective-permute-start | bytes 98312 | tf_op jit(solution)/shard_map/ppermute | solution.py:223
  12.6 1.4 %collective-permute-done.6 = bf16[32,512]{1,0:T(8,128)(2,1)S(1)} collective-permute-done((bf16[32,512]{1,0:T(8,128)(2,1)S(1)}, bf16[32,512]{1,0:T(8,128)(2,1)S(1)}, u32[]{:S(2)}, u32[]{:S(2)}) %collective-permute-start.6) | collective-permute-done | bytes 32800 | tf_op jit(solution)/shard_map/ppermute | solution.py:223
  14.0 1.3 %collective-permute-start.7 = (bf16[64,512]{1,0:T(8,128)(2,1)S(1)}, bf16[64,512]{1,0:T(8,128)(2,1)S(1)}, u32[]{:S(2)}, u32[]{:S(2)}) collective-permute-start(bf16[64,512]{1,0:T(8,128)(2,1)S(1)} %pad_maximum_fusion), channel_id=1, source_target_pairs={{0,16},{1,17},{2,18},{3,19},{4,20},{5,21},{6,22},{7,23},{8,40},{9,... | collective-permute-start | bytes 196616 | tf_op jit(solution)/shard_map/ppermute | solution.py:223
  15.3 1.8 %collective-permute-done.7 = bf16[64,512]{1,0:T(8,128)(2,1)S(1)} collective-permute-done((bf16[64,512]{1,0:T(8,128)(2,1)S(1)}, bf16[64,512]{1,0:T(8,128)(2,1)S(1)}, u32[]{:S(2)}, u32[]{:S(2)}) %collective-permute-start.7) | collective-permute-done | bytes 65568 | tf_op jit(solution)/shard_map/ppermute | solution.py:223
  17.1 5.4 %collective-permute-start.8 = (bf16[128,512]{1,0:T(8,128)(2,1)S(1)}, bf16[128,512]{1,0:T(8,128)(2,1)S(1)}, u32[]{:S(2)}, u32[]{:S(2)}) collective-permute-start(bf16[128,512]{1,0:T(8,128)(2,1)S(1)} %constant_dynamic-update-slice_fusion.refs_4_), channel_id=1, source_target_pairs={{0,8},{1,9},{2,10},{3,11},{4,12},{5,13},{6,14},{7,15},{8,0},{9,1},... | collective-permute-start | bytes 393224 | tf_op jit(solution)/shard_map/ppermute | solution.py:223
  22.5 0.7 %collective-permute-start.4 = (bf16[32,512]{1,0:T(8,128)(2,1)S(1)}, bf16[32,512]{1,0:T(8,128)(2,1)S(1)}, u32[]{:S(2)}, u32[]{:S(2)}) collective-permute-start(bf16[32,512]{1,0:T(8,128)(2,1)S(1)} %pad_maximum_fusion.2.refs_0_), channel_id=1, source_target_pairs={{0,6},{1,7},{2,4},{3,5},{4,2},{5,3},{6,0},{7,1},{8,14},{9,15},{10,... | collective-permute-start | bytes 98312 | tf_op jit(solution)/shard_map/ppermute | solution.py:223
  23.2 2.0 %collective-permute-start.3 = (bf16[32,512]{1,0:T(8,128)(2,1)S(1)}, bf16[32,512]{1,0:T(8,128)(2,1)S(1)}, u32[]{:S(2)}, u32[]{:S(2)}) collective-permute-start(bf16[32,512]{1,0:T(8,128)(2,1)S(1)} %pad_maximum_fusion.2.refs_0_), channel_id=1, source_target_pairs={{0,4},{1,5},{2,6},{3,7},{4,0},{5,1},{6,2},{7,3},{8,12},{9,13},{10,... | collective-permute-start | bytes 98312 | tf_op jit(solution)/shard_map/ppermute | solution.py:223
  25.2 0.6 %collective-permute-start.2 = (bf16[32,512]{1,0:T(8,128)(2,1)S(1)}, bf16[32,512]{1,0:T(8,128)(2,1)S(1)}, u32[]{:S(2)}, u32[]{:S(2)}) collective-permute-start(bf16[32,512]{1,0:T(8,128)(2,1)S(1)} %pad_maximum_fusion.2.refs_0_), channel_id=1, source_target_pairs={{0,2},{1,3},{2,0},{3,1},{4,6},{5,7},{6,4},{7,5},{8,10},{9,11},{10,... | collective-permute-start | bytes 98312 | tf_op jit(solution)/shard_map/ppermute | solution.py:223
  25.8 0.7 %collective-permute-done.4.refs_3_ = bf16[32,512]{1,0:T(8,128)(2,1)S(1)} collective-permute-done((bf16[32,512]{1,0:T(8,128)(2,1)S(1)}, bf16[32,512]{1,0:T(8,128)(2,1)S(1)}, u32[]{:S(2)}, u32[]{:S(2)}) %collective-permute-start.4) | collective-permute-done | bytes 32800 | tf_op jit(solution)/shard_map/ppermute | solution.py:223
  26.5 1.0 %collective-permute-done.3.refs_2_ = bf16[32,512]{1,0:T(8,128)(2,1)S(1)} collective-permute-done((bf16[32,512]{1,0:T(8,128)(2,1)S(1)}, bf16[32,512]{1,0:T(8,128)(2,1)S(1)}, u32[]{:S(2)}, u32[]{:S(2)}) %collective-permute-start.3) | collective-permute-done | bytes 32800 | tf_op jit(solution)/shard_map/ppermute | solution.py:223
  27.5 1.1 %collective-permute-done.2.refs_1_ = bf16[32,512]{1,0:T(8,128)(2,1)S(1)} collective-permute-done((bf16[32,512]{1,0:T(8,128)(2,1)S(1)}, bf16[32,512]{1,0:T(8,128)(2,1)S(1)}, u32[]{:S(2)}, u32[]{:S(2)}) %collective-permute-start.2) | collective-permute-done | bytes 32800 | tf_op jit(solution)/shard_map/ppermute | solution.py:223
  28.6 0.0 collective-permute-done.8.refs_5_
  28.6 3.4 %correlate.1 = f32[51,128,256]{2,1,0:T(8,128)} custom-call(bf16[32,512]{1,0:T(8,128)(2,1)S(1)} %pad_maximum_fusion.2.refs_0_, bf16[32,512]{1,0:T(8,128)(2,1)S(1)} %collective-permute-done.2.refs_1_, bf16[32,512]{1,0:T(8,128)(2,1)S(1)} %collective-permute-done.3.refs_2_, bf16[32,512]{1,0:T(8,128)(2,1)S(1)} %collective-permute-done.4.refs_3_, ...), custom_call_target="tpu_custom_call" | custom-call | flops 2147483648 | bytes 8388608 | tf_op jit(solution)/shard_map/correlate/pallas_call | solution.py:200
  (6 shorter events, 0.0 us)
Async XLA Ops:
  1.8 2.3 %collective-permute-start.1 = (bf16[16,512]{1,0:T(8,128)(2,1)S(1)}, bf16[16,512]{1,0:T(8,128)(2,1)S(1)}, u32[]{:S(2)}, u32[]{:S(2)}) collective-permute-start(bf16[16,512]{1,0:T(8,128)(2,1)S(1)} %whiten.1), channel_id=1, source_target_pairs={{0,8},{1,9},{2,10},{3,11},{4,12},{5,13},{6,14},{7,15},{8,0},{9,1},... | collective-permute-start | bytes 49160 | tf_op jit(solution)/shard_map/ppermute | solution.py:223
  4.1 5.7 %collective-permute-start.5 = (bf16[32,512]{1,0:T(8,128)(2,1)S(1)}, bf16[32,512]{1,0:T(8,128)(2,1)S(1)}, u32[]{:S(2)}, u32[]{:S(2)}) collective-permute-start(bf16[32,512]{1,0:T(8,128)(2,1)S(1)} %pad_maximum_fusion.1), channel_id=1, source_target_pairs={{0,64},{1,80},{2,96},{3,112},{4,0},{5,16},{6,32},{7,48},{8,40},{9,... | collective-permute-start | bytes 98312 | tf_op jit(solution)/shard_map/ppermute | solution.py:223
  5.5 4.3 %collective-permute-start = (bf16[16,512]{1,0:T(8,128)(2,1)S(1)}, bf16[16,512]{1,0:T(8,128)(2,1)S(1)}, u32[]{:S(2)}, u32[]{:S(2)}) collective-permute-start(bf16[16,512]{1,0:T(8,128)(2,1)S(1)} %whiten.1), channel_id=1, source_target_pairs={{0,1},{1,0},{2,3},{3,2},{4,5},{5,4},{6,7},{7,6},{8,9},{9,8},{10,11... | collective-permute-start | bytes 49160 | tf_op jit(solution)/shard_map/ppermute | solution.py:223
  9.8 4.2 %collective-permute-start.6 = (bf16[32,512]{1,0:T(8,128)(2,1)S(1)}, bf16[32,512]{1,0:T(8,128)(2,1)S(1)}, u32[]{:S(2)}, u32[]{:S(2)}) collective-permute-start(bf16[32,512]{1,0:T(8,128)(2,1)S(1)} %collective-permute-done.5), channel_id=1, source_target_pairs={{0,32},{1,33},{2,34},{3,35},{4,36},{5,37},{6,38},{7,39},{8,24},{9,... | collective-permute-start | bytes 98312 | tf_op jit(solution)/shard_map/ppermute | solution.py:223
  14.0 3.1 %collective-permute-start.7 = (bf16[64,512]{1,0:T(8,128)(2,1)S(1)}, bf16[64,512]{1,0:T(8,128)(2,1)S(1)}, u32[]{:S(2)}, u32[]{:S(2)}) collective-permute-start(bf16[64,512]{1,0:T(8,128)(2,1)S(1)} %pad_maximum_fusion), channel_id=1, source_target_pairs={{0,16},{1,17},{2,18},{3,19},{4,20},{5,21},{6,22},{7,23},{8,40},{9,... | collective-permute-start | bytes 196616 | tf_op jit(solution)/shard_map/ppermute | solution.py:223
  17.1 11.5 %collective-permute-start.8 = (bf16[128,512]{1,0:T(8,128)(2,1)S(1)}, bf16[128,512]{1,0:T(8,128)(2,1)S(1)}, u32[]{:S(2)}, u32[]{:S(2)}) collective-permute-start(bf16[128,512]{1,0:T(8,128)(2,1)S(1)} %constant_dynamic-update-slice_fusion.refs_4_), channel_id=1, source_target_pairs={{0,8},{1,9},{2,10},{3,11},{4,12},{5,13},{6,14},{7,15},{8,0},{9,1},... | collective-permute-start | bytes 393224 | tf_op jit(solution)/shard_map/ppermute | solution.py:223
  22.5 4.0 %collective-permute-start.4 = (bf16[32,512]{1,0:T(8,128)(2,1)S(1)}, bf16[32,512]{1,0:T(8,128)(2,1)S(1)}, u32[]{:S(2)}, u32[]{:S(2)}) collective-permute-start(bf16[32,512]{1,0:T(8,128)(2,1)S(1)} %pad_maximum_fusion.2.refs_0_), channel_id=1, source_target_pairs={{0,6},{1,7},{2,4},{3,5},{4,2},{5,3},{6,0},{7,1},{8,14},{9,15},{10,... | collective-permute-start | bytes 98312 | tf_op jit(solution)/shard_map/ppermute | solution.py:223
  23.2 4.3 %collective-permute-start.3 = (bf16[32,512]{1,0:T(8,128)(2,1)S(1)}, bf16[32,512]{1,0:T(8,128)(2,1)S(1)}, u32[]{:S(2)}, u32[]{:S(2)}) collective-permute-start(bf16[32,512]{1,0:T(8,128)(2,1)S(1)} %pad_maximum_fusion.2.refs_0_), channel_id=1, source_target_pairs={{0,4},{1,5},{2,6},{3,7},{4,0},{5,1},{6,2},{7,3},{8,12},{9,13},{10,... | collective-permute-start | bytes 98312 | tf_op jit(solution)/shard_map/ppermute | solution.py:223
  25.2 3.4 %collective-permute-start.2 = (bf16[32,512]{1,0:T(8,128)(2,1)S(1)}, bf16[32,512]{1,0:T(8,128)(2,1)S(1)}, u32[]{:S(2)}, u32[]{:S(2)}) collective-permute-start(bf16[32,512]{1,0:T(8,128)(2,1)S(1)} %pad_maximum_fusion.2.refs_0_), channel_id=1, source_target_pairs={{0,2},{1,3},{2,0},{3,1},{4,6},{5,7},{6,4},{7,5},{8,10},{9,11},{10,... | collective-permute-start | bytes 98312 | tf_op jit(solution)/shard_map/ppermute | solution.py:223
